TPU v7x, 32 devices: a whole 2x2x4 slice. The times are simulated.
32 devices in a mesh: ctx: 8 (over y, x, core), head: 4 (over z).
Axes of the slice: x: 2, y: 2, z: 4, core: 2. Of those that a mesh axis runs over, the one named last changes fastest.
Arguments:
- queries: bfloat16 [8192, 8, 128], P(('ctx', 'head')), may hold values from -4.5 to 4.5
- keys_in: bfloat16 [8192, 8, 128], P(('ctx', 'head')), may hold values from -4.5 to 4.5
- values: bfloat16 [8192, 8, 128], P(('ctx', 'head')), may hold values from -6 to 6
- grad_out: bfloat16 [8192, 8, 128], P(('ctx', 'head')), may hold values from -6 to 6
- slopes: float32 [8], replicated, may hold values from 0.00024414062 to 0.03125
- doc_lengths: int32 [16], replicated, may hold values from 1 to 1024, 8192 in all
Outputs:
- grad_query: bfloat16 [8192, 8, 128], P(('ctx', 'head'))
- grad_key: bfloat16 [8192, 8, 128], P(('ctx', 'head'))
- grad_value: bfloat16 [8192, 8, 128], P(('ctx', 'head'))
Inputs may be any that keep to these rules, and one draw needn't show every extreme that they name: `doc_lengths`: the 16 lengths sum to 8192, and the longest is exactly 1024.
All inputs are finite; a program needn't handle non-finite values.
Results may differ from a plain program's by a relative error of at most 0.0075.
Values may be sent and summed in bfloat16 or wider, within the bound.
A program may use at most 64 MiB of HBM per device.

v0:
```python
from functools import partial
import math

import jax
import jax.numpy as jnp
from jax import lax
from jax.experimental import pallas as pl
from jax.experimental.pallas import tpu as pltpu
from jax.sharding import PartitionSpec as P

F32 = jnp.float32
BF16 = jnp.bfloat16
VMEM_ALL = 65208320
LOG2E = math.log2(math.e)
NT = (((1,), (1,)), ((), ()))
NN = (((1,), (0,)), ((), ()))
TN = (((0,), (0,)), ((), ()))


def repeat(count, step):
    if count <= 8:
        for n in range(count):
            step(n)
    else:

        def looped(n, carry):
            step(n)
            return carry

        lax.fori_loop(0, count, looped, 0)


def kernel(
    sizes,
    k_hbm, v_hbm, q_hbm, g_hbm, slope_hbm, doc_hbm,
    dq_hbm, dk_hbm, dv_hbm,
    k_raw, v_raw, q_raw, g_raw, k_in, v_in, q_in, g_in, dq_out, dk_out, dv_out, slope_ref, doc_ref, low_ref,
    k_all, v_all, q_all, g_all,
    s_buf, dp_buf, top, low_sum, weighted, dq_acc, dk_acc, dv_acc,
    dq_mine, dk_mine, dv_mine, dk_part, dv_part, dk_got, dv_got,
    small_sem, raw_sem, own_sem, in_send, in_recv, fwd_send, fwd_recv, back_send, back_recv, out_send, out_recv,
):
    n_head, n_ctx, reach, here, tok, rows, depth, tile = sizes
    z = lax.axis_index("head")
    c = lax.axis_index("ctx")
    past = reach * rows
    chunks = (past + tile) // tile
    inv_scale = 1.0 / math.sqrt(depth)

    def peer(off):
        other, bit = z, 1
        while bit < n_head:
            if off & bit:
                other = other + bit * (1 - 2 * lax.rem(z // bit, 2))
            bit *= 2
        return other

    offs = tuple(range(1, n_head))

    def along(off):
        return lax.rem(c + off + n_ctx, n_ctx)

    wholes = (k_hbm, v_hbm, q_hbm, g_hbm)
    raws = (k_raw, v_raw, q_raw, g_raw)

    def raw_copy(a):
        return pltpu.make_async_copy(wholes[a], raws[a], raw_sem.at[a])

    for a in range(4):
        raw_copy(a).start()
    small = (
        pltpu.make_async_copy(slope_hbm, slope_ref, small_sem.at[0]),
        pltpu.make_async_copy(doc_hbm, doc_ref, small_sem.at[1]),
    )
    for copy in small:
        copy.start()

    barrier = pltpu.get_barrier_semaphore()
    for off in range(1, n_head):
        pl.semaphore_signal(barrier, inc=1, device_id={"head": peer(off)}, device_id_type=pl.DeviceIdType.MESH)
    for off in range(1, reach + 1):
        for side in (off, -off):
            pl.semaphore_signal(barrier, inc=1, device_id={"ctx": along(side)}, device_id_type=pl.DeviceIdType.MESH)

    sources = (k_in, v_in, q_in, g_in)
    holders = (k_all, v_all, q_all, g_all)
    bases = (past, past, 0, 0)

    def own_copy(i, a):
        return pltpu.make_async_copy(
            sources[a].at[z * here + i],
            holders[a].at[i, pl.ds(pl.multiple_of(bases[a] + z * tok, tok), tok)],
            own_sem.at[i, a],
        )

    def in_copy(i, a, off):
        return pltpu.make_async_remote_copy(
            src_ref=sources[a].at[peer(off) * here + i],
            dst_ref=holders[a].at[i, pl.ds(pl.multiple_of(bases[a] + z * tok, tok), tok)],
            send_sem=in_send.at[i, a, off - 1],
            recv_sem=in_recv.at[i, a, off - 1],
            device_id={"head": peer(off)},
            device_id_type=pl.DeviceIdType.MESH,
        )

    def fwd_copy(i, a, r):
        return pltpu.make_async_remote_copy(
            src_ref=holders[a].at[i, pl.ds(past, rows)],
            dst_ref=holders[a].at[i, pl.ds((reach - r) * rows, rows)],
            send_sem=fwd_send.at[i, a, r - 1],
            recv_sem=fwd_recv.at[i, a, r - 1],
            device_id={"ctx": along(r)},
            device_id_type=pl.DeviceIdType.MESH,
        )

    parts = (dk_part, dv_part)
    gots = (dk_got, dv_got)

    def back_copy(i, a, r):
        return pltpu.make_async_remote_copy(
            src_ref=parts[a].at[i, pl.ds((reach - r) * rows, rows)],
            dst_ref=gots[a].at[i, r - 1],
            send_sem=back_send.at[i, a, r - 1],
            recv_sem=back_recv.at[i, a, r - 1],
            device_id={"ctx": along(-r)},
            device_id_type=pl.DeviceIdType.MESH,
        )

    mine = (dq_mine, dk_mine, dv_mine)
    outs = (dq_out, dk_out, dv_out)

    def out_copy(i, a, off):
        return pltpu.make_async_remote_copy(
            src_ref=mine[a].at[i, pl.ds(pl.multiple_of(peer(off) * tok, tok), tok)],
            dst_ref=outs[a].at[z * here + i],
            send_sem=out_send.at[i, a, off - 1],
            recv_sem=out_recv.at[i, a, off - 1],
            device_id={"head": peer(off)},
            device_id_type=pl.DeviceIdType.MESH,
        )

    def send_out(i, a):
        for off in offs:
            out_copy(i, a, off).start()
        outs[a][z * here + i] = mine[a][i, pl.ds(pl.multiple_of(z * tok, tok), tok)]

    def arrived(i, a):
        own_copy(i, a).wait()
        for off in range(1, n_head):
            in_copy(i, a, off).wait_recv()

    def attend(i):
        slope2 = slope_ref[z * here + i] * LOG2E
        dk_acc[...] = jnp.zeros_like(dk_acc)
        dv_acc[...] = jnp.zeros_like(dv_acc)

        def block(b, carry):
            first = pl.multiple_of(b * tile, tile)
            q = q_all[i, pl.ds(first, tile)]
            g = g_all[i, pl.ds(first, tile)]
            low = low_ref[:, pl.ds(first, tile)] + (past - first).astype(F32)
            high = past + lax.broadcasted_iota(jnp.int32, (1, tile), 1)
            high = high.astype(F32)
            spot = lax.broadcasted_iota(jnp.int32, (tile, tile), 0).astype(F32)
            top[...] = jnp.full_like(top, -1e30)
            low_sum[...] = jnp.zeros_like(low_sum)
            weighted[...] = jnp.zeros_like(weighted)
            dq_acc[...] = jnp.zeros_like(dq_acc)

            def window(n):
                return pl.ds(pl.multiple_of(first + n * tile, tile), tile)

            def held(n):
                return pl.ds(pl.multiple_of(n * tile, tile), tile)

            def score(n):
                raw = lax.dot_general(k_all[i, window(n)], q, NT, preferred_element_type=F32)
                where = spot + jnp.float32(n * tile)
                s = raw * (inv_scale * LOG2E) + slope2 * (where - past)
                s = jnp.where((where >= low) & (where <= high), s, -1e30)
                s_buf[held(n)] = s
                top[...] = jnp.maximum(top[...], jnp.max(s, axis=0, keepdims=True))

            def weigh(n):
                p = jnp.exp2(s_buf[held(n)] - top[...])
                dp = lax.dot_general(v_all[i, window(n)], g, NT, preferred_element_type=F32)
                s_buf[held(n)] = p
                dp_buf[held(n)] = dp
                low_sum[...] += jnp.sum(p, axis=0, keepdims=True)
                weighted[...] += jnp.sum(p * dp, axis=0, keepdims=True)

            repeat(chunks, score)
            repeat(chunks, weigh)
            share = 1.0 / low_sum[...]
            delta = weighted[...] * share

            def spread(n):
                w = s_buf[held(n)] * share
                ds = (w * (dp_buf[held(n)] - delta)).astype(BF16)
                dv_acc[window(n)] += lax.dot_general(w.astype(BF16), g, NN, preferred_element_type=F32)
                dk_acc[window(n)] += lax.dot_general(ds, q, NN, preferred_element_type=F32)
                dq_acc[...] += lax.dot_general(k_all[i, window(n)], ds, TN, preferred_element_type=F32)

            repeat(chunks, spread)
            dq_mine[i, pl.ds(first, tile)] = (dq_acc[...] * inv_scale).T.astype(BF16)
            return carry

        lax.fori_loop(0, rows // tile, block, 0)
        dk_part[i] = dk_acc[pl.ds(0, past)].astype(BF16)
        dv_part[i] = dv_acc[pl.ds(0, past)].astype(BF16)

    def settle(i, a, acc, scale):
        total = acc
        for r in range(1, reach + 1):
            back_copy(i, a, r).wait_recv()
            total = total + gots[a][i, r - 1].astype(F32)
        mine[1 + a][i] = (total * scale).astype(BF16)
        send_out(i, 1 + a)

    def start_head(i, a):
        for off in offs:
            in_copy(i, a, off).start()
        own_copy(i, a).start()

    def turn(source, target, count):
        if source.shape[0] == tok:
            for n in range(0, tok, count):
                target[:, n : n + count] = jnp.swapaxes(source[n : n + count], 0, 1)
        else:
            for n in range(0, tok, count):
                target[n : n + count] = jnp.swapaxes(source[:, n : n + count], 0, 1)

    step = min(64, tok)
    for a in range(4):
        raw_copy(a).wait()
        turn(raws[a], sources[a], step)
        if a == 0:
            pl.semaphore_wait(barrier, n_head - 1 + 2 * reach)
        start_head(0, a)
    for i in range(1, here):
        for a in range(4):
            start_head(i, a)

    for copy in small:
        copy.wait()
    spots = lax.broadcasted_iota(jnp.int32, (1, rows), 1) + c * rows
    start = jnp.int32(0)
    low = jnp.zeros((1, rows), jnp.int32)
    for n in range(doc_ref.shape[0]):
        low = jnp.where(spots >= start, start, low)
        start = start + doc_ref[n]
    low_ref[...] = (low - c * rows).astype(F32)

    def forward(i):
        for a in range(2):
            arrived(i, a)
            for r in range(1, reach + 1):
                fwd_copy(i, a, r).start()

    forward(0)
    for i in range(here):
        for a in (2, 3):
            arrived(i, a)
        for a in range(2):
            for r in range(1, reach + 1):
                fwd_copy(i, a, r).wait_recv()
        attend(i)
        for a in range(2):
            for r in range(1, reach + 1):
                back_copy(i, a, r).start()
        send_out(i, 0)
        if i + 1 < here:
            forward(i + 1)
        settle(i, 0, dk_acc[pl.ds(past, rows)], inv_scale)
        settle(i, 1, dv_acc[pl.ds(past, rows)], 1.0)

    results = (dq_hbm, dk_hbm, dv_hbm)

    def result_copy(a):
        return pltpu.make_async_copy(raws[a], results[a], raw_sem.at[a])

    for a in range(3):
        for i in range(here):
            for off in offs:
                out_copy(i, a, off).wait_recv()
        turn(outs[a], raws[a], step)
        result_copy(a).start()

    for i in range(here):
        for off in offs:
            for a in range(4):
                in_copy(i, a, off).wait_send()
            for a in range(3):
                out_copy(i, a, off).wait_send()
        for a in range(2):
            for r in range(1, reach + 1):
                fwd_copy(i, a, r).wait_send()
                back_copy(i, a, r).wait_send()
    for a in range(3):
        result_copy(a).wait()


def hand_over(a_in, b_in, c_in, a_out, b_out, c_out, a_buf, b_buf, c_buf, in_sem, out_sem):
    bufs = (a_buf, b_buf, c_buf)
    ins = [pltpu.make_async_copy(x, bufs[n], in_sem.at[n]) for n, x in enumerate((a_in, b_in, c_in))]
    outs = [pltpu.make_async_copy(bufs[n], x, out_sem.at[n]) for n, x in enumerate((a_out, b_out, c_out))]
    for copy in ins:
        copy.start()
    for arrive, leave in zip(ins, outs):
        arrive.wait()
        leave.start()
    for copy in outs:
        copy.wait()


def body(queries, keys_in, values, grad_out, slopes, doc_lengths):
    n_head = lax.axis_size("head")
    n_ctx = lax.axis_size("ctx")
    tok, heads, depth = queries.shape
    here = heads // n_head
    rows = tok * n_head
    span = min(16384, rows * n_ctx // 8)
    reach = span // rows
    past = reach * rows
    tile = min(256, rows)
    sizes = (n_head, n_ctx, reach, here, tok, rows, depth, tile)
    away = pl.BlockSpec(memory_space=pl.ANY)
    dma = pltpu.SemaphoreType.DMA
    out = jax.ShapeDtypeStruct((tok, heads, depth), BF16)
    swapped = pltpu.VMEM((heads, tok, depth), BF16)
    window = past + tile
    pairs = rows * window * here
    grads = pl.pallas_call(
        partial(kernel, sizes),
        out_shape=(out, out, out),
        in_specs=[away] * 6,
        out_specs=(away,) * 3,
        scratch_shapes=[pltpu.VMEM((tok, heads, depth), BF16)] * 4
        + [swapped] * 7
        + [
            pltpu.SMEM(slopes.shape, F32),
            pltpu.SMEM(doc_lengths.shape, jnp.int32),
            pltpu.VMEM((1, rows), F32),
            pltpu.VMEM((here, past + rows, depth), BF16),
            pltpu.VMEM((here, past + rows, depth), BF16),
            pltpu.VMEM((here, rows, depth), BF16),
            pltpu.VMEM((here, rows, depth), BF16),
            pltpu.VMEM((window, tile), F32),
            pltpu.VMEM((window, tile), F32),
            pltpu.VMEM((1, tile), F32),
            pltpu.VMEM((1, tile), F32),
            pltpu.VMEM((1, tile), F32),
            pltpu.VMEM((depth, tile), F32),
            pltpu.VMEM((past + rows, depth), F32),
            pltpu.VMEM((past + rows, depth), F32),
            pltpu.VMEM((here, rows, depth), BF16),
            pltpu.VMEM((here, rows, depth), BF16),
            pltpu.VMEM((here, rows, depth), BF16),
            pltpu.VMEM((here, past, depth), BF16),
            pltpu.VMEM((here, past, depth), BF16),
            pltpu.VMEM((here, reach, rows, depth), BF16),
            pltpu.VMEM((here, reach, rows, depth), BF16),
            dma((2,)),
            dma((4,)),
            dma((here, 4)),
            dma((here, 4, n_head - 1)),
            dma((here, 4, n_head - 1)),
            dma((here, 2, reach)),
            dma((here, 2, reach)),
            dma((here, 2, reach)),
            dma((here, 2, reach)),
            dma((here, 3, n_head - 1)),
            dma((here, 3, n_head - 1)),
        ],
        compiler_params=pltpu.CompilerParams(
            collective_id=0, has_side_effects=True, vmem_limit_bytes=VMEM_ALL
        ),
        cost_estimate=pl.CostEstimate(
            flops=10 * pairs * depth, bytes_accessed=14 * heads * tok * depth, transcendentals=pairs
        ),
    )(keys_in, values, queries, grad_out, slopes, doc_lengths)
    return pl.pallas_call(
        hand_over,
        out_shape=(out, out, out),
        in_specs=[away] * 3,
        out_specs=(away,) * 3,
        scratch_shapes=[pltpu.VMEM((tok, heads, depth), BF16)] * 3 + [dma((3,)), dma((3,))],
        compiler_params=pltpu.CompilerParams(vmem_limit_bytes=VMEM_ALL),
    )(*grads)


def solution(mesh):
    placed = P(("ctx", "head"), None, None)
    return jax.shard_map(
        body,
        mesh=mesh,
        in_specs=(placed, placed, placed, placed, P(), P()),
        out_specs=(placed, placed, placed),
        check_vma=False,
    )
```

profile of v0, /device:TPU:0, one launch (start us, length us, event | category | flops | bytes accessed | tf_op | source)
XLA Modules:
  0.0 89.2 jit_solution(7921188087368235408)
XLA Ops:
  0.6 86.3 %shard_map.85 = (bf16[256,8,128]{2,1,0:T(8,128)(2,1)}, bf16[256,8,128]{2,1,0:T(8,128)(2,1)}, bf16[256,8,128]{2,1,0:T(8,128)(2,1)}) custom-call(bf16[256,8,128]{2,1,0:T(8,128)(2,1)} %k_hbm.1, bf16[256,8,128]{2,1,0:T(8,128)(2,1)} %v_hbm.1, bf16[256,8,128]{2,1,0:T(8,128)(2,1)} %q_hbm.1, bf16[256,8,128]{2,1,0:T(8,128)(2,1)} %g_hbm.1, f32[8]{0:T(128)} %slope_hbm.1, ...), custom_call_target="tpu_custom_call" | custom-call | flops 3355443200 | bytes 3670016 | tf_op jit(solution)/shard_map/pallas_call | solution.py:333
  87.0 2.2 %shard_map.86 = (bf16[256,8,128]{2,1,0:T(8,128)(2,1)}, bf16[256,8,128]{2,1,0:T(8,128)(2,1)}, bf16[256,8,128]{2,1,0:T(8,128)(2,1)}) custom-call(bf16[256,8,128]{2,1,0:T(8,128)(2,1)} %get-tuple-element.6.a_in, bf16[256,8,128]{2,1,0:T(8,128)(2,1)} %get-tuple-element.7.b_in, bf16[256,8,128]{2,1,0:T(8,128)(2,1)} %get-tuple-element.8.c_in), custom_call_target="tpu_custom_call" | custom-call | tf_op jit(solution)/shard_map/pallas_call | solution.py:382
where the time goes:
time: 89.4 us; the launch traced here: 89.2 us
  Pallas kernels  88.6 us (99%)
    pallas_call x1, Pallas kernels, body(): pl.pallas_call(partial(kernel, sizes), out_shape=(out, out, out), in_spec...  86.3 us
    pallas_call x1, Pallas kernels, body(): pl.pallas_call(hand_over, out_shape=(out, out, out), in_specs=[away] * 3,...  2.23 us

commit v1 on v0

--- a/solution.py
+++ b/solution.py
@@ -298,6 +298,463 @@
                 back_copy(i, a, r).wait_send()
     for a in range(3):
         result_copy(a).wait()
+
+
+def chain_kernel(
+    sizes,
+    k_hbm, v_hbm, q_hbm, g_hbm, slope_hbm, doc_hbm,
+    dq_hbm, dk_hbm, dv_hbm,
+    k_raw, v_raw, q_raw, g_raw, k_in, v_in, q_in, g_in, dq_out, dk_out, dv_out, slope_ref, doc_ref, low_ref,
+    k_all, v_all, q_all, g_all,
+    p_buf, dp_buf, top, stat, stat_got, both, dq_acc, dk_acc, dv_acc, dq_rows,
+    dq_own, dq_next, dq_far, got_next, got_far, got_side, dq_pair, dk_pair, dv_pair, got_pair,
+    small_sem, raw_sem, own_sem, in_send, in_recv, near_send, near_recv, far_send, far_recv,
+    stat_send, stat_recv, next_send, next_recv, side_recv, back_send, back_recv, pair_send, pair_recv,
+):
+    n_ctx, mine, tok, depth = sizes
+    z = lax.axis_index("head")
+    c = lax.axis_index("ctx")
+    side = z // 2
+    half = lax.rem(z, 2)
+    rest = 1 - half
+    chunk = 2 * tok
+    span = 3 * chunk
+    first_key = (2 * c + side) * chunk
+    inner = lax.rem(side + half, 2) == 1
+    outer = lax.rem(side + half, 2) == 0
+    inv_scale = 1.0 / math.sqrt(depth)
+
+    before, after = lax.rem(c - 1 + n_ctx, n_ctx), lax.rem(c + 1, n_ctx)
+    c_less = lax.rem(c - (1 - side) + n_ctx, n_ctx)
+    c_more = lax.rem(c + side, n_ctx)
+    across = z + 2 - 4 * side
+    mirror = 3 - z
+    twin = {"head": z + 1 - 2 * half}
+    less_one, more_one = {"ctx": c_less, "head": across}, {"ctx": c_more, "head": across}
+    less_mirror, more_mirror = {"ctx": c_less, "head": mirror}, {"ctx": c_more, "head": mirror}
+    less_two, more_two = {"ctx": before}, {"ctx": after}
+
+    def remote(src, dst, send, recv, device):
+        return pltpu.make_async_remote_copy(
+            src_ref=src, dst_ref=dst, send_sem=send, recv_sem=recv,
+            device_id=device, device_id_type=pl.DeviceIdType.MESH,
+        )
+
+    wholes = (k_hbm, v_hbm, q_hbm, g_hbm)
+    raws = (k_raw, v_raw, q_raw, g_raw)
+    sources = (k_in, v_in, q_in, g_in)
+    holders = (k_all, v_all, q_all, g_all)
+
+    def raw_copy(a):
+        return pltpu.make_async_copy(wholes[a], raws[a], raw_sem.at[a])
+
+    for a in (2, 3, 0, 1):
+        raw_copy(a).start()
+    small = (
+        pltpu.make_async_copy(slope_hbm, slope_ref, small_sem.at[0]),
+        pltpu.make_async_copy(doc_hbm, doc_ref, small_sem.at[1]),
+    )
+    for copy in small:
+        copy.start()
+
+    barrier = pltpu.get_barrier_semaphore()
+    peers = (twin, less_one, more_one, less_mirror, more_mirror, less_two, more_two)
+    for device in peers:
+        pl.semaphore_signal(barrier, inc=1, device_id=device, device_id_type=pl.DeviceIdType.MESH)
+
+    def block(base, which):
+        return pl.ds(pl.multiple_of(base + which * tok, tok), tok)
+
+    def own_copy(i, a):
+        return pltpu.make_async_copy(sources[a].at[half * mine + i], holders[a].at[i, block(0, half)], own_sem.at[i, a])
+
+    def in_copy(i, a):
+        return remote(
+            sources[a].at[rest * mine + i], holders[a].at[i, block(0, half)], in_send.at[i, a], in_recv.at[i, a], twin
+        )
+
+    def near_own(i, a):
+        return remote(
+            sources[a].at[half * mine + i], holders[a].at[i, block(chunk, half)],
+            near_send.at[i, a - 2, 0], near_recv.at[i, a - 2, half], less_one,
+        )
+
+    def near_other(i, a):
+        return remote(
+            sources[a].at[rest * mine + i], holders[a].at[i, block(chunk, half)],
+            near_send.at[i, a - 2, 1], near_recv.at[i, a - 2, half], less_mirror,
+        )
+
+    def near_relay(i, a):
+        return remote(
+            holders[a].at[i, block(0, rest)], holders[a].at[i, block(chunk, rest)],
+            near_send.at[i, a - 2, 2], near_recv.at[i, a - 2, rest], less_one,
+        )
+
+    def far_copy(i, a):
+        return remote(
+            holders[a].at[i, pl.ds(0, chunk)], holders[a].at[i, pl.ds(2 * chunk, chunk)],
+            far_send.at[i, a - 2], far_recv.at[i, a - 2], less_two,
+        )
+
+    routes = (
+        (0, less_one, 1, 0),
+        (0, less_two, 2, 0),
+        (1, more_one, 0, 0),
+        (1, less_one, 2, 1),
+        (2, more_two, 0, 1),
+        (2, more_one, 1, 1),
+    )
+
+    def stat_copy(i, m):
+        slot, device, there, place = routes[m]
+        return remote(
+            stat.at[i, slot], stat_got.at[i, there, place], stat_send.at[i, m], stat_recv.at[i, there, place], device
+        )
+
+    def next_own(i):
+        return remote(
+            dq_next.at[i, block(0, half)], got_next.at[i], next_send.at[i, 0], next_recv.at[i], more_one
+        )
+
+    def next_side(i):
+        kind = lax.rem(side + half + 1, 2)
+        device = {"ctx": c_more, "head": 2 - side}
+        return remote(
+            dq_next.at[i, block(0, rest)], got_side.at[kind, i], next_send.at[i, 1], side_recv.at[kind, i], device
+        )
+
+    def back_copy(i):
+        return remote(dq_far.at[i], got_far.at[i], back_send.at[i], back_recv.at[i], more_two)
+
+    pairs = (dq_pair, dk_pair, dv_pair)
+    pair_targets = (None, dk_out, dv_out)
+
+    def pair_copy(i, a):
+        target = got_pair.at[i] if a == 0 else pair_targets[a].at[half * mine + i]
+        return remote(pairs[a].at[i], target, pair_send.at[i, a], pair_recv.at[i, a], twin)
+
+    def pair_wait(i, a):
+        target = got_pair.at[i] if a == 0 else pair_targets[a].at[rest * mine + i]
+        remote(pairs[a].at[i], target, pair_send.at[i, a], pair_recv.at[i, a], twin).wait_recv()
+
+    step = min(64, tok)
+
+    def turn(source, target):
+        if source.shape[0] == tok:
+            for n in range(0, tok, step):
+                target[:, n : n + step] = jnp.swapaxes(source[n : n + step], 0, 1)
+        else:
+            for n in range(0, tok, step):
+                target[n : n + step] = jnp.swapaxes(source[:, n : n + step], 0, 1)
+
+    def open_head(i, a):
+        in_copy(i, a).start()
+        own_copy(i, a).start()
+        if a >= 2:
+            near_own(i, a).start()
+
+            @pl.when(inner)
+            def _():
+                near_other(i, a).start()
+
+    def relay(i):
+        for a in (2, 3):
+            own_copy(i, a).wait()
+            in_copy(i, a).wait_recv()
+            far_copy(i, a).start()
+
+            @pl.when(inner)
+            def _():
+                near_relay(i, a).start()
+
+    def arrived(i):
+        for a in (0, 1):
+            own_copy(i, a).wait()
+            in_copy(i, a).wait_recv()
+        for a in (2, 3):
+            far_copy(i, a).wait_recv()
+            near_own(i, a).wait_recv()
+            near_relay(i, a).wait_recv()
+
+    def tile_rows(t):
+        return pl.ds(pl.multiple_of(t * tok, tok), tok)
+
+    def gather(i, slot_of):
+        slope2 = slope_ref[half * mine + i] * LOG2E
+
+        def slot_step(slot, carry):
+            for u in range(2):
+                t = 2 * slot + u
+                q = q_all[i, tile_rows(t)]
+                g = g_all[i, tile_rows(t)]
+                low = low_ref[:, tile_rows(t)]
+                first = (t * tok).astype(F32)
+                high = lax.broadcasted_iota(jnp.int32, (1, tok), 1).astype(F32) + first
+                spot = lax.broadcasted_iota(jnp.int32, (tok, tok), 0).astype(F32)
+                best = jnp.full((1, tok), -1e30, F32)
+                for b in range(2):
+                    raw = lax.dot_general(k_all[i, b * tok : (b + 1) * tok], q, NT, preferred_element_type=F32)
+                    where = spot + jnp.float32(b * tok)
+                    s = raw * (inv_scale * LOG2E) + slope2 * (where - first)
+                    s = jnp.where((where >= low) & (where <= high), s, -1e30)
+                    p_buf[slot_of, t, b] = s
+                    best = jnp.maximum(best, jnp.max(s, axis=0, keepdims=True))
+                total = jnp.zeros((1, tok), F32)
+                weighted = jnp.zeros((1, tok), F32)
+                for b in range(2):
+                    p = jnp.exp2(p_buf[slot_of, t, b] - best)
+                    dp = lax.dot_general(v_all[i, b * tok : (b + 1) * tok], g, NT, preferred_element_type=F32)
+                    p_buf[slot_of, t, b] = p
+                    dp_buf[slot_of, t, b] = dp
+                    total = total + jnp.sum(p, axis=0, keepdims=True)
+                    weighted = weighted + jnp.sum(p * dp, axis=0, keepdims=True)
+                top[slot_of, t] = best
+                level = best + jnp.log2(total)
+                share = weighted / total
+                for r in range(lanes):
+                    row = u * lanes + r
+                    part = slice(r * depth, (r + 1) * depth)
+                    stat[i, slot, row : row + 1] = level[:, part]
+                    stat[i, slot, 2 * lanes + row : 2 * lanes + row + 1] = share[:, part]
+            return carry
+
+        lax.fori_loop(0, 3, slot_step, 0)
+        for m in range(6):
+            stat_copy(i, m).start()
+
+    lanes = tok // depth
+
+    def spread(i, slot_of):
+        for slot in range(3):
+            for place in range(2):
+                remote(
+                    stat.at[i, slot], stat_got.at[i, slot, place], stat_send.at[i, 0], stat_recv.at[i, slot, place], twin
+                ).wait_recv()
+            found = (stat[i, slot], stat_got[i, slot, 0], stat_got[i, slot, 1])
+            levels = [x[: 2 * lanes] for x in found]
+            shares = [x[2 * lanes :] for x in found]
+            peak = jnp.maximum(jnp.maximum(levels[0], levels[1]), levels[2])
+            full = peak + jnp.log2(sum(jnp.exp2(x - peak) for x in levels))
+            delta = sum(jnp.exp2(x - full) * y for x, y in zip(levels, shares))
+            for u in range(2):
+                for r in range(lanes):
+                    row = u * lanes + r
+                    part = slice(r * depth, (r + 1) * depth)
+                    both[0, 2 * slot + u, :, part] = full[row : row + 1]
+                    both[1, 2 * slot + u, :, part] = delta[row : row + 1]
+        dk_acc[...] = jnp.zeros_like(dk_acc)
+        dv_acc[...] = jnp.zeros_like(dv_acc)
+
+        def tile_step(t, carry):
+            q = q_all[i, tile_rows(t)]
+            g = g_all[i, tile_rows(t)]
+            share = jnp.exp2(top[slot_of, t] - both[0, t])
+            delta = both[1, t]
+            for b in range(2):
+                rows = slice(b * tok, (b + 1) * tok)
+                w = p_buf[slot_of, t, b] * share
+                ds = (w * (dp_buf[slot_of, t, b] - delta)).astype(BF16)
+                dv_acc[rows] += lax.dot_general(w.astype(BF16), g, NN, preferred_element_type=F32)
+                dk_acc[rows] += lax.dot_general(ds, q, NN, preferred_element_type=F32)
+                part = lax.dot_general(k_all[i, rows], ds, TN, preferred_element_type=F32)
+                if b == 0:
+                    dq_acc[...] = part
+                else:
+                    dq_acc[...] += part
+            dq_rows[tile_rows(t)] = (dq_acc[...] * inv_scale).T
+            return carry
+
+        lax.fori_loop(0, 6, tile_step, 0)
+        dq_next[i] = dq_rows[chunk : 2 * chunk].astype(BF16)
+        next_side(i).start()
+        next_own(i).start()
+        dq_far[i] = dq_rows[2 * chunk : 3 * chunk].astype(BF16)
+        back_copy(i).start()
+        dq_own[i] = dq_rows[0:chunk]
+        dk_pair[i] = (dk_acc[block(0, rest)] * inv_scale).astype(BF16)
+        pair_copy(i, 1).start()
+        dv_pair[i] = dv_acc[block(0, rest)].astype(BF16)
+        pair_copy(i, 2).start()
+        dk_out[half * mine + i] = (dk_acc[block(0, half)] * inv_scale).astype(BF16)
+        dv_out[half * mine + i] = dv_acc[block(0, half)].astype(BF16)
+
+    def settle(i):
+        back_copy(i).wait_recv()
+
+        @pl.when(inner)
+        def _():
+            remote(dq_pair.at[i], got_side.at[1, i], next_send.at[i, 1], side_recv.at[1, i], twin).wait_recv()
+
+        dq_pair[i] = (
+            dq_own[i, block(0, rest)] + got_far[i, block(0, rest)].astype(F32) + got_side[1, i].astype(F32)
+        ).astype(BF16)
+        pair_copy(i, 0).start()
+        next_own(i).wait_recv()
+        dq_out[half * mine + i] = (
+            dq_own[i, block(0, half)] + got_far[i, block(0, half)].astype(F32) + got_next[i].astype(F32)
+        ).astype(BF16)
+
+    def close(i):
+        pair_wait(i, 0)
+
+        @pl.when(inner)
+        def _():
+            remote(dq_pair.at[i], got_side.at[0, i], next_send.at[i, 1], side_recv.at[0, i], twin).wait_recv()
+
+        dq_out[rest * mine + i] = (got_pair[i].astype(F32) + got_side[0, i].astype(F32)).astype(BF16)
+
+    for a in (2, 3, 0, 1):
+        raw_copy(a).wait()
+        turn(raws[a], sources[a])
+        if a == 2:
+            pl.semaphore_wait(barrier, len(peers))
+        open_head(0, a)
+    for a in (2, 3, 0, 1):
+        if mine > 1:
+            open_head(1, a)
+
+    @pl.when(outer)
+    def _():
+        got_side[...] = jnp.zeros_like(got_side)
+
+    for copy in small:
+        copy.wait()
+    spots = lax.broadcasted_iota(jnp.int32, (1, span), 1) + first_key
+    start = jnp.int32(0)
+    low = jnp.zeros((1, span), jnp.int32)
+    for n in range(doc_ref.shape[0]):
+        low = jnp.where(spots >= start, start, low)
+        start = start + doc_ref[n]
+    low = jnp.where(spots >= start, spots + 1, low)
+    low_ref[...] = (low - first_key).astype(F32)
+
+    relay(0)
+    for i in range(mine):
+        if i + 1 < mine:
+            relay(i + 1)
+        if i + 2 < mine:
+            for a in (2, 3, 0, 1):
+                open_head(i + 2, a)
+        arrived(i)
+        gather(i, i % 2)
+        if i >= 1:
+            spread(i - 1, (i - 1) % 2)
+        if i >= 2:
+            settle(i - 2)
+    spread(mine - 1, (mine - 1) % 2)
+    for i in range(max(0, mine - 2), mine):
+        settle(i)
+
+    results = (dq_hbm, dk_hbm, dv_hbm)
+    outs = (dq_out, dk_out, dv_out)
+
+    def result_copy(a):
+        return pltpu.make_async_copy(raws[a], results[a], raw_sem.at[a])
+
+    for a in (1, 2):
+        for i in range(mine):
+            pair_wait(i, a)
+        turn(outs[a], raws[a])
+        result_copy(a).start()
+    for i in range(mine):
+        close(i)
+    turn(outs[0], raws[0])
+    result_copy(0).start()
+
+    for i in range(mine):
+        for a in range(4):
+            in_copy(i, a).wait_send()
+        for a in (2, 3):
+            near_own(i, a).wait_send()
+            far_copy(i, a).wait_send()
+        for m in range(6):
+            stat_copy(i, m).wait_send()
+        next_own(i).wait_send()
+        next_side(i).wait_send()
+        back_copy(i).wait_send()
+        for a in range(3):
+            pair_copy(i, a).wait_send()
+
+    @pl.when(inner)
+    def _():
+        for i in range(mine):
+            for a in (2, 3):
+                near_other(i, a).wait_send()
+                near_relay(i, a).wait_send()
+
+    for a in range(3):
+        result_copy(a).wait()
+
+
+def chain_call(n_ctx, tok, heads, depth, slots, docs):
+    mine = heads // 2
+    chunk = 2 * tok
+    away = pl.BlockSpec(memory_space=pl.ANY)
+    dma = pltpu.SemaphoreType.DMA
+    out = jax.ShapeDtypeStruct((tok, heads, depth), BF16)
+    pairs = mine * 6 * chunk * tok
+    return pl.pallas_call(
+        partial(chain_kernel, (n_ctx, mine, tok, depth)),
+        out_shape=(out, out, out),
+        in_specs=[away] * 6,
+        out_specs=(away,) * 3,
+        scratch_shapes=[pltpu.VMEM((tok, heads, depth), BF16)] * 4
+        + [pltpu.VMEM((heads, tok, depth), BF16)] * 7
+        + [
+            pltpu.SMEM(slots, F32),
+            pltpu.SMEM(docs, jnp.int32),
+            pltpu.VMEM((1, 3 * chunk), F32),
+            pltpu.VMEM((mine, chunk, depth), BF16),
+            pltpu.VMEM((mine, chunk, depth), BF16),
+            pltpu.VMEM((mine, 3 * chunk, depth), BF16),
+            pltpu.VMEM((mine, 3 * chunk, depth), BF16),
+            pltpu.VMEM((2, 6, 2, tok, tok), F32),
+            pltpu.VMEM((2, 6, 2, tok, tok), F32),
+            pltpu.VMEM((2, 6, 1, tok), F32),
+            pltpu.VMEM((mine, 3, 4 * tok // depth, depth), F32),
+            pltpu.VMEM((mine, 3, 2, 4 * tok // depth, depth), F32),
+            pltpu.VMEM((2, 6, 1, tok), F32),
+            pltpu.VMEM((depth, tok), F32),
+            pltpu.VMEM((chunk, depth), F32),
+            pltpu.VMEM((chunk, depth), F32),
+            pltpu.VMEM((3 * chunk, depth), F32),
+            pltpu.VMEM((mine, chunk, depth), F32),
+            pltpu.VMEM((mine, chunk, depth), BF16),
+            pltpu.VMEM((mine, chunk, depth), BF16),
+            pltpu.VMEM((mine, tok, depth), BF16),
+            pltpu.VMEM((mine, chunk, depth), BF16),
+            pltpu.VMEM((2, mine, tok, depth), BF16),
+            pltpu.VMEM((mine, tok, depth), BF16),
+            pltpu.VMEM((mine, tok, depth), BF16),
+            pltpu.VMEM((mine, tok, depth), BF16),
+            pltpu.VMEM((mine, tok, depth), BF16),
+            dma((2,)),
+            dma((4,)),
+            dma((mine, 4)),
+            dma((mine, 4)),
+            dma((mine, 4)),
+            dma((mine, 2, 3)),
+            dma((mine, 2, 2)),
+            dma((mine, 2)),
+            dma((mine, 2)),
+            dma((mine, 6)),
+            dma((mine, 3, 2)),
+            dma((mine, 2)),
+            dma((mine,)),
+            dma((2, mine)),
+            dma((mine,)),
+            dma((mine,)),
+            dma((mine, 3)),
+            dma((mine, 3)),
+        ],
+        compiler_params=pltpu.CompilerParams(
+            collective_id=1, has_side_effects=True, vmem_limit_bytes=VMEM_ALL
+        ),
+        cost_estimate=pl.CostEstimate(
+            flops=10 * pairs * depth, bytes_accessed=14 * heads * tok * depth, transcendentals=pairs
+        ),
+    )
 
 
 def hand_over(a_in, b_in, c_in, a_out, b_out, c_out, a_buf, b_buf, c_buf, in_sem, out_sem):
@@ -330,7 +787,7 @@
     swapped = pltpu.VMEM((heads, tok, depth), BF16)
     window = past + tile
     pairs = rows * window * here
-    grads = pl.pallas_call(
+    call = pl.pallas_call(
         partial(kernel, sizes),
         out_shape=(out, out, out),
         in_specs=[away] * 6,
@@ -378,7 +835,10 @@
         cost_estimate=pl.CostEstimate(
             flops=10 * pairs * depth, bytes_accessed=14 * heads * tok * depth, transcendentals=pairs
         ),
-    )(keys_in, values, queries, grad_out, slopes, doc_lengths)
+    )
+    if n_head == 4 and past == rows and heads % 2 == 0 and tok % (2 * depth) == 0:
+        call = chain_call(n_ctx, tok, heads, depth, slopes.shape, doc_lengths.shape)
+    grads = call(keys_in, values, queries, grad_out, slopes, doc_lengths)
     return pl.pallas_call(
         hand_over,
         out_shape=(out, out, out),

time: 89.4 us -> 90 us (level)
  no operation moved by 1% of the time
where the time goes in v1:
time: 90 us; the launch traced here: 89.8 us
  Pallas kernels  89.2 us (99%)
    pallas_call x1, Pallas kernels, body(): grads = call(keys_in, values, queries, grad_out, slopes, doc_lengths)  86.9 us
    pallas_call x1, Pallas kernels, body(): pl.pallas_call(hand_over, out_shape=(out, out, out), in_specs=[away] * 3,...  2.23 us

profile of v1, /device:TPU:0, one launch (start us, length us, event | category | flops | bytes accessed | tf_op | source)
XLA Modules:
  0.0 89.8 jit_solution(17262284877277257567)
XLA Ops:
  0.6 86.9 %shard_map.85 = (bf16[256,8,128]{2,1,0:T(8,128)(2,1)}, bf16[256,8,128]{2,1,0:T(8,128)(2,1)}, bf16[256,8,128]{2,1,0:T(8,128)(2,1)}) custom-call(bf16[256,8,128]{2,1,0:T(8,128)(2,1)} %k_hbm.1, bf16[256,8,128]{2,1,0:T(8,128)(2,1)} %v_hbm.1, bf16[256,8,128]{2,1,0:T(8,128)(2,1)} %q_hbm.1, bf16[256,8,128]{2,1,0:T(8,128)(2,1)} %g_hbm.1, f32[8]{0:T(128)} %slope_hbm.1, ...), custom_call_target="tpu_custom_call" | custom-call | flops 4026531840 | bytes 3670016 | tf_op jit(solution)/shard_map/pallas_call | solution.py:841
  87.6 2.2 %shard_map.86 = (bf16[256,8,128]{2,1,0:T(8,128)(2,1)}, bf16[256,8,128]{2,1,0:T(8,128)(2,1)}, bf16[256,8,128]{2,1,0:T(8,128)(2,1)}) custom-call(bf16[256,8,128]{2,1,0:T(8,128)(2,1)} %get-tuple-element.6.a_in, bf16[256,8,128]{2,1,0:T(8,128)(2,1)} %get-tuple-element.7.b_in, bf16[256,8,128]{2,1,0:T(8,128)(2,1)} %get-tuple-element.8.c_in), custom_call_target="tpu_custom_call" | custom-call | tf_op jit(solution)/shard_map/pallas_call | solution.py:842

commit v2 on v1

--- a/solution.py
+++ b/solution.py
@@ -358,9 +358,17 @@
         copy.start()
 
     barrier = pltpu.get_barrier_semaphore()
-    peers = (twin, less_one, more_one, less_mirror, more_mirror, less_two, more_two)
-    for device in peers:
+
+    def greet(device):
         pl.semaphore_signal(barrier, inc=1, device_id=device, device_id_type=pl.DeviceIdType.MESH)
+
+    greet(more_one)
+    greet(more_two)
+    greet(twin)
+
+    @pl.when(inner)
+    def _():
+        greet(more_mirror)
 
     def block(base, which):
         return pl.ds(pl.multiple_of(base + which * tok, tok), tok)
@@ -567,8 +575,6 @@
 
         lax.fori_loop(0, 6, tile_step, 0)
         dq_next[i] = dq_rows[chunk : 2 * chunk].astype(BF16)
-        next_side(i).start()
-        next_own(i).start()
         dq_far[i] = dq_rows[2 * chunk : 3 * chunk].astype(BF16)
         back_copy(i).start()
         dq_own[i] = dq_rows[0:chunk]
@@ -579,6 +585,10 @@
         dk_out[half * mine + i] = (dk_acc[block(0, half)] * inv_scale).astype(BF16)
         dv_out[half * mine + i] = dv_acc[block(0, half)].astype(BF16)
 
+    def send_next(i):
+        next_side(i).start()
+        next_own(i).start()
+
     def settle(i):
         back_copy(i).wait_recv()
 
@@ -608,7 +618,7 @@
         raw_copy(a).wait()
         turn(raws[a], sources[a])
         if a == 2:
-            pl.semaphore_wait(barrier, len(peers))
+            pl.semaphore_wait(barrier, 3 + lax.rem(side + half, 2))
         open_head(0, a)
     for a in (2, 3, 0, 1):
         if mine > 1:
@@ -630,20 +640,32 @@
     low_ref[...] = (low - first_key).astype(F32)
 
     relay(0)
+    if mine > 1:
+        relay(1)
+    held = []
     for i in range(mine):
-        if i + 1 < mine:
-            relay(i + 1)
         if i + 2 < mine:
             for a in (2, 3, 0, 1):
                 open_head(i + 2, a)
         arrived(i)
         gather(i, i % 2)
+        for m in held:
+            send_next(m)
+        held = []
         if i >= 1:
             spread(i - 1, (i - 1) % 2)
-        if i >= 2:
-            settle(i - 2)
+            held = [i - 1]
+        if i + 2 < mine:
+            relay(i + 2)
+        if i + 3 >= mine and i + 1 < mine and i + 2 < mine:
+            for m in held:
+                send_next(m)
+            held = []
+    for m in held:
+        send_next(m)
     spread(mine - 1, (mine - 1) % 2)
-    for i in range(max(0, mine - 2), mine):
+    send_next(mine - 1)
+    for i in range(mine):
         settle(i)
 
     results = (dq_hbm, dk_hbm, dv_hbm)

time: 90 us -> 87.2 us (0.969)
  Pallas kernels: 89.2 us -> 86.1 us
    pallas_call x1, Pallas kernels: 86.9 us -> 83.9 us  [body(): grads = call(keys_in, values, queries, grad_out, slopes, doc_lengths)]
where the time goes in v2:
time: 87.2 us; the launch traced here: 86.8 us
  Pallas kernels  86.1 us (99%)
    pallas_call x1, Pallas kernels, body(): grads = call(keys_in, values, queries, grad_out, slopes, doc_lengths)  83.9 us
    pallas_call x1, Pallas kernels, body(): pl.pallas_call(hand_over, out_shape=(out, out, out), in_specs=[away] * 3,...  2.23 us

profile of v2, /device:TPU:0, one launch (start us, length us, event | category | flops | bytes accessed | tf_op | source)
XLA Modules:
  0.0 86.8 jit_solution(2425215453047741873)
XLA Ops:
  0.6 83.9 %shard_map.85 = (bf16[256,8,128]{2,1,0:T(8,128)(2,1)}, bf16[256,8,128]{2,1,0:T(8,128)(2,1)}, bf16[256,8,128]{2,1,0:T(8,128)(2,1)}) custom-call(bf16[256,8,128]{2,1,0:T(8,128)(2,1)} %k_hbm.1, bf16[256,8,128]{2,1,0:T(8,128)(2,1)} %v_hbm.1, bf16[256,8,128]{2,1,0:T(8,128)(2,1)} %q_hbm.1, bf16[256,8,128]{2,1,0:T(8,128)(2,1)} %g_hbm.1, f32[8]{0:T(128)} %slope_hbm.1, ...), custom_call_target="tpu_custom_call" | custom-call | flops 4026531840 | bytes 3670016 | tf_op jit(solution)/shard_map/pallas_call | solution.py:863
  84.5 2.2 %shard_map.86 = (bf16[256,8,128]{2,1,0:T(8,128)(2,1)}, bf16[256,8,128]{2,1,0:T(8,128)(2,1)}, bf16[256,8,128]{2,1,0:T(8,128)(2,1)}) custom-call(bf16[256,8,128]{2,1,0:T(8,128)(2,1)} %get-tuple-element.6.a_in, bf16[256,8,128]{2,1,0:T(8,128)(2,1)} %get-tuple-element.7.b_in, bf16[256,8,128]{2,1,0:T(8,128)(2,1)} %get-tuple-element.8.c_in), custom_call_target="tpu_custom_call" | custom-call | tf_op jit(solution)/shard_map/pallas_call | solution.py:864

commit v3 on v2

--- a/solution.py
+++ b/solution.py
@@ -11,6 +11,7 @@
 F32 = jnp.float32
 BF16 = jnp.bfloat16
 VMEM_ALL = 65208320
+VMEM_PART = 48 << 20
 LOG2E = math.log2(math.e)
 NT = (((1,), (1,)), ((), ()))
 NN = (((1,), (0,)), ((), ()))
@@ -303,8 +304,8 @@
 def chain_kernel(
     sizes,
     k_hbm, v_hbm, q_hbm, g_hbm, slope_hbm, doc_hbm,
-    dq_hbm, dk_hbm, dv_hbm,
-    k_raw, v_raw, q_raw, g_raw, k_in, v_in, q_in, g_in, dq_out, dk_out, dv_out, slope_ref, doc_ref, low_ref,
+    dq_out, dk_out, dv_out,
+    k_raw, v_raw, q_raw, g_raw, k_in, v_in, q_in, g_in, slope_ref, doc_ref, low_ref,
     k_all, v_all, q_all, g_all,
     p_buf, dp_buf, top, stat, stat_got, both, dq_acc, dk_acc, dv_acc, dq_rows,
     dq_own, dq_next, dq_far, got_next, got_far, got_side, dq_pair, dk_pair, dv_pair, got_pair,
@@ -449,12 +450,8 @@
     step = min(64, tok)
 
     def turn(source, target):
-        if source.shape[0] == tok:
-            for n in range(0, tok, step):
-                target[:, n : n + step] = jnp.swapaxes(source[n : n + step], 0, 1)
-        else:
-            for n in range(0, tok, step):
-                target[n : n + step] = jnp.swapaxes(source[:, n : n + step], 0, 1)
+        for n in range(0, tok, step):
+            target[:, n : n + step] = jnp.swapaxes(source[n : n + step], 0, 1)
 
     def open_head(i, a):
         in_copy(i, a).start()
@@ -668,21 +665,11 @@
     for i in range(mine):
         settle(i)
 
-    results = (dq_hbm, dk_hbm, dv_hbm)
-    outs = (dq_out, dk_out, dv_out)
-
-    def result_copy(a):
-        return pltpu.make_async_copy(raws[a], results[a], raw_sem.at[a])
-
     for a in (1, 2):
         for i in range(mine):
             pair_wait(i, a)
-        turn(outs[a], raws[a])
-        result_copy(a).start()
     for i in range(mine):
         close(i)
-    turn(outs[0], raws[0])
-    result_copy(0).start()
 
     for i in range(mine):
         for a in range(4):
@@ -705,24 +692,22 @@
                 near_other(i, a).wait_send()
                 near_relay(i, a).wait_send()
 
-    for a in range(3):
-        result_copy(a).wait()
-
 
 def chain_call(n_ctx, tok, heads, depth, slots, docs):
     mine = heads // 2
     chunk = 2 * tok
-    away = pl.BlockSpec(memory_space=pl.ANY)
+    away = pl.BlockSpec(memory_space=pltpu.MemorySpace.HBM)
     dma = pltpu.SemaphoreType.DMA
-    out = jax.ShapeDtypeStruct((tok, heads, depth), BF16)
+    out = jax.ShapeDtypeStruct((heads, tok, depth), BF16)
+    near = pl.BlockSpec(memory_space=pltpu.VMEM)
     pairs = mine * 6 * chunk * tok
     return pl.pallas_call(
         partial(chain_kernel, (n_ctx, mine, tok, depth)),
         out_shape=(out, out, out),
         in_specs=[away] * 6,
-        out_specs=(away,) * 3,
+        out_specs=(near,) * 3,
         scratch_shapes=[pltpu.VMEM((tok, heads, depth), BF16)] * 4
-        + [pltpu.VMEM((heads, tok, depth), BF16)] * 7
+        + [pltpu.VMEM((heads, tok, depth), BF16)] * 4
         + [
             pltpu.SMEM(slots, F32),
             pltpu.SMEM(docs, jnp.int32),
@@ -771,12 +756,25 @@
             dma((mine, 3)),
         ],
         compiler_params=pltpu.CompilerParams(
-            collective_id=1, has_side_effects=True, vmem_limit_bytes=VMEM_ALL
+            collective_id=1, has_side_effects=True, vmem_limit_bytes=VMEM_PART
         ),
         cost_estimate=pl.CostEstimate(
             flops=10 * pairs * depth, bytes_accessed=14 * heads * tok * depth, transcendentals=pairs
         ),
     )
+
+
+def turn_over(a_in, b_in, c_in, a_out, b_out, c_out, a_buf, b_buf, c_buf, sem):
+    tok = a_buf.shape[0]
+    step = min(64, tok)
+    copies = []
+    for m, (x, buf, y) in enumerate(((b_in, b_buf, b_out), (c_in, c_buf, c_out), (a_in, a_buf, a_out))):
+        for n in range(0, tok, step):
+            buf[n : n + step] = jnp.swapaxes(x[:, n : n + step], 0, 1)
+        copies.append(pltpu.make_async_copy(buf, y, sem.at[m]))
+        copies[-1].start()
+    for copy in copies:
+        copy.wait()
 
 
 def hand_over(a_in, b_in, c_in, a_out, b_out, c_out, a_buf, b_buf, c_buf, in_sem, out_sem):
@@ -790,6 +788,10 @@
         leave.start()
     for copy in outs:
         copy.wait()
+
+
+def stay(x):
+    return pltpu.with_memory_space_constraint(x, pltpu.MemorySpace.HBM)
 
 
 def body(queries, keys_in, values, grad_out, slopes, doc_lengths):
@@ -860,6 +862,15 @@
     )
     if n_head == 4 and past == rows and heads % 2 == 0 and tok % (2 * depth) == 0:
         call = chain_call(n_ctx, tok, heads, depth, slopes.shape, doc_lengths.shape)
+        near = pl.BlockSpec(memory_space=pltpu.VMEM)
+        return pl.pallas_call(
+            turn_over,
+            out_shape=(out, out, out),
+            in_specs=[near] * 3,
+            out_specs=(away,) * 3,
+            scratch_shapes=[pltpu.VMEM((tok, heads, depth), BF16)] * 3 + [dma((3,))],
+            compiler_params=pltpu.CompilerParams(vmem_limit_bytes=VMEM_PART),
+        )(*call(*(stay(x) for x in (keys_in, values, queries, grad_out, slopes, doc_lengths))))
     grads = call(keys_in, values, queries, grad_out, slopes, doc_lengths)
     return pl.pallas_call(
         hand_over,

time: 87.2 us -> 85.4 us (0.979)
  Pallas kernels: 86.1 us -> 84.4 us
    pallas_call x2, Pallas kernels: 86.1 us -> 84.4 us  [the longest x1 83.1 us: body(): call(*(stay(x) for x in (keys_in, values, queries, grad_out, slopes, doc_...]
where the time goes in v3:
time: 85.4 us; the launch traced here: 85 us
  Pallas kernels  84.4 us (99%)
    pallas_call x1, Pallas kernels, body(): call(*(stay(x) for x in (keys_in, values, queries, grad_out, slopes, doc_...  83.1 us

profile of v3, /device:TPU:0, one launch (start us, length us, event | category | flops | bytes accessed | tf_op | source)
XLA Modules:
  0.0 85.0 jit_solution(9310474247773690415)
XLA Ops:
  0.6 83.1 %shard_map.85 = (bf16[8,256,128]{2,1,0:T(8,128)(2,1)S(1)}, bf16[8,256,128]{2,1,0:T(8,128)(2,1)S(1)}, bf16[8,256,128]{2,1,0:T(8,128)(2,1)S(1)}) custom-call(bf16[256,8,128]{2,1,0:T(8,128)(2,1)} %k_hbm.1, bf16[256,8,128]{2,1,0:T(8,128)(2,1)} %v_hbm.1, bf16[256,8,128]{2,1,0:T(8,128)(2,1)} %q_hbm.1, bf16[256,8,128]{2,1,0:T(8,128)(2,1)} %g_hbm.1, f32[8]{0:T(128)} %slope_hbm.1, ...), custom_call_target="tpu_custom_call" | custom-call | flops 4026531840 | bytes 3670016 | tf_op jit(solution)/shard_map/pallas_call | solution.py:873
  83.7 1.3 %shard_map.86 = (bf16[256,8,128]{2,1,0:T(8,128)(2,1)}, bf16[256,8,128]{2,1,0:T(8,128)(2,1)}, bf16[256,8,128]{2,1,0:T(8,128)(2,1)}) custom-call(bf16[8,256,128]{2,1,0:T(8,128)(2,1)S(1)} %get-tuple-element.6.a_in, bf16[8,256,128]{2,1,0:T(8,128)(2,1)S(1)} %get-tuple-element.7.b_in, bf16[8,256,128]{2,1,0:T(8,128)(2,1)S(1)} %get-tuple-element.8.c_in), custom_call_target="tpu_custom_call" | custom-call | tf_op jit(solution)/shard_map/pallas_call | solution.py:866

commit v4 on v3

--- a/solution.py
+++ b/solution.py
@@ -427,6 +427,10 @@
         )
 
     def next_side(i):
+        if i == mine - 1:
+            return remote(
+                dq_next.at[i, block(0, rest)], got_side.at[0, i], next_send.at[i, 1], side_recv.at[0, i], more_mirror
+            )
         kind = lax.rem(side + half + 1, 2)
         device = {"ctx": c_more, "head": 2 - side}
         return remote(
@@ -588,15 +592,18 @@
 
     def settle(i):
         back_copy(i).wait_recv()
-
-        @pl.when(inner)
-        def _():
-            remote(dq_pair.at[i], got_side.at[1, i], next_send.at[i, 1], side_recv.at[1, i], twin).wait_recv()
-
-        dq_pair[i] = (
-            dq_own[i, block(0, rest)] + got_far[i, block(0, rest)].astype(F32) + got_side[1, i].astype(F32)
-        ).astype(BF16)
+        passed = dq_own[i, block(0, rest)] + got_far[i, block(0, rest)].astype(F32)
+        if i < mine - 1:
+
+            @pl.when(inner)
+            def _():
+                remote(dq_pair.at[i], got_side.at[1, i], next_send.at[i, 1], side_recv.at[1, i], twin).wait_recv()
+
+            passed = passed + got_side[1, i].astype(F32)
+        dq_pair[i] = passed.astype(BF16)
         pair_copy(i, 0).start()
+
+    def finish(i):
         next_own(i).wait_recv()
         dq_out[half * mine + i] = (
             dq_own[i, block(0, half)] + got_far[i, block(0, half)].astype(F32) + got_next[i].astype(F32)
@@ -604,10 +611,11 @@
 
     def close(i):
         pair_wait(i, 0)
-
-        @pl.when(inner)
-        def _():
-            remote(dq_pair.at[i], got_side.at[0, i], next_send.at[i, 1], side_recv.at[0, i], twin).wait_recv()
+        side_copy = remote(dq_pair.at[i], got_side.at[0, i], next_send.at[i, 1], side_recv.at[0, i], twin)
+        if i == mine - 1:
+            side_copy.wait_recv()
+        else:
+            pl.when(inner)(side_copy.wait_recv)
 
         dq_out[rest * mine + i] = (got_pair[i].astype(F32) + got_side[0, i].astype(F32)).astype(BF16)
 
@@ -623,7 +631,8 @@
 
     @pl.when(outer)
     def _():
-        got_side[...] = jnp.zeros_like(got_side)
+        for i in range(mine - 1):
+            got_side[:, i] = jnp.zeros((2, tok, depth), BF16)
 
     for copy in small:
         copy.wait()
@@ -640,10 +649,10 @@
     if mine > 1:
         relay(1)
     held = []
+    for i in range(2, mine):
+        for a in (2, 3, 0, 1):
+            open_head(i, a)
     for i in range(mine):
-        if i + 2 < mine:
-            for a in (2, 3, 0, 1):
-                open_head(i + 2, a)
         arrived(i)
         gather(i, i % 2)
         for m in held:
@@ -654,16 +663,14 @@
             held = [i - 1]
         if i + 2 < mine:
             relay(i + 2)
-        if i + 3 >= mine and i + 1 < mine and i + 2 < mine:
-            for m in held:
-                send_next(m)
-            held = []
     for m in held:
         send_next(m)
     spread(mine - 1, (mine - 1) % 2)
     send_next(mine - 1)
     for i in range(mine):
         settle(i)
+    for i in range(mine):
+        finish(i)
 
     for a in (1, 2):
         for i in range(mine):

time: 85.4 us -> 83.6 us (0.979)
  Pallas kernels: 84.4 us -> 82.7 us
    pallas_call x1, Pallas kernels: 83.1 us -> 81.4 us  [body(): call(*(stay(x) for x in (keys_in, values, queries, grad_out, slopes, doc_...]
where the time goes in v4:
time: 83.6 us; the launch traced here: 83.4 us
  Pallas kernels  82.7 us (99%)
    pallas_call x1, Pallas kernels, body(): call(*(stay(x) for x in (keys_in, values, queries, grad_out, slopes, doc_...  81.4 us

profile of v4, /device:TPU:0, one launch (start us, length us, event | category | flops | bytes accessed | tf_op | source)
XLA Modules:
  0.0 83.4 jit_solution(3983606384065147402)
XLA Ops:
  0.6 81.4 %shard_map.85 = (bf16[8,256,128]{2,1,0:T(8,128)(2,1)S(1)}, bf16[8,256,128]{2,1,0:T(8,128)(2,1)S(1)}, bf16[8,256,128]{2,1,0:T(8,128)(2,1)S(1)}) custom-call(bf16[256,8,128]{2,1,0:T(8,128)(2,1)} %k_hbm.1, bf16[256,8,128]{2,1,0:T(8,128)(2,1)} %v_hbm.1, bf16[256,8,128]{2,1,0:T(8,128)(2,1)} %q_hbm.1, bf16[256,8,128]{2,1,0:T(8,128)(2,1)} %g_hbm.1, f32[8]{0:T(128)} %slope_hbm.1, ...), custom_call_target="tpu_custom_call" | custom-call | flops 4026531840 | bytes 3670016 | tf_op jit(solution)/shard_map/pallas_call | solution.py:880
  82.0 1.3 %shard_map.86 = (bf16[256,8,128]{2,1,0:T(8,128)(2,1)}, bf16[256,8,128]{2,1,0:T(8,128)(2,1)}, bf16[256,8,128]{2,1,0:T(8,128)(2,1)}) custom-call(bf16[8,256,128]{2,1,0:T(8,128)(2,1)S(1)} %get-tuple-element.6.a_in, bf16[8,256,128]{2,1,0:T(8,128)(2,1)S(1)} %get-tuple-element.7.b_in, bf16[8,256,128]{2,1,0:T(8,128)(2,1)S(1)} %get-tuple-element.8.c_in), custom_call_target="tpu_custom_call" | custom-call | tf_op jit(solution)/shard_map/pallas_call | solution.py:873
